TPU v7x, 128 devices: a whole 4x4x4 slice. The times are simulated.
128 devices in a mesh: req: 16 (over z, x), mlp: 8 (over y, core).
Axes of the slice: x: 4, y: 4, z: 4, core: 2. Of those that a mesh axis runs over, the one named last changes fastest.
Arguments:
- tokens: bfloat16 [65536, 1024], P(('req', 'mlp')), may hold values from -72 to 72
- attend_weight: bfloat16 [1024, 3072], replicated, may hold values from -0.1875 to 0.1875
- output_weight: bfloat16 [1024, 1024], replicated, may hold values from -0.1875 to 0.1875
- attend_gain: float32 [1024], replicated, may hold values from 0.1 to 1.9
- up_weight: bfloat16 [1024, 4096], P(None, 'mlp'), may hold values from -0.1875 to 0.1875
- down_weight: bfloat16 [1024, 4096], P(None, 'mlp'), may hold values from -0.09375 to 0.09375
- mlp_gain: float32 [1024], replicated, may hold values from 0.1 to 1.9
- embed_weight: bfloat16 [1024, 128], replicated, may hold values from -0.1875 to 0.1875
- query_length: int32 [512], P(('req', 'mlp')), may hold values from 1 to 128, 49152 in all
- documents: bfloat16 [128, 256, 128], P('req', 'mlp'), may hold values from -0.54 to 0.54
- document_length: int32 [128], P('req'), may hold values from 1 to 256, 16512 in all
- candidates: int32 [512, 8], P(('req', 'mlp')), may hold values from 0 to 127
Outputs:
- embedded: bfloat16 [65536, 128], P(('req', 'mlp'))
- scores: float32 [512, 8], P(('req', 'mlp'))
All inputs are finite; a program needn't handle non-finite values. No bound on the sum of `query_length` or of `document_length` on one device may be relied on, other than what follows from the above.
Results may differ from a plain program's by a relative error of at most 0.015.
The roundings to bfloat16 on the way count: a program that leaves them out, or rounds other values in their place, can miss the bound.
Values may be sent and summed in bfloat16 or wider, within the bound.
No kernel may reach another device: no remote copies, remote signals or barrier semaphores. Data moves between devices by JAX's collectives and lax.ppermute only.
A program may use at most 128 MiB of HBM per device.

v0:
```python
import jax
import jax.numpy as jnp
from jax import lax
from jax.sharding import PartitionSpec as P

D = 1024
HEADS = 16
HD = 64
P_SIZE = 128
SEQ = 128


def norm_rows(values, scaling):
    average = jnp.mean(values, axis=-1, keepdims=True)
    centred = values - average
    variance = jnp.mean(centred * centred, axis=-1, keepdims=True)
    return centred * lax.rsqrt(variance + 1e-05) * scaling


def best_match(piece, flat_docs, live_doc):
    sims = lax.dot_general(
        piece, flat_docs, (((1,), (1,)), ((), ())), preferred_element_type=jnp.float32
    )
    sims = sims.reshape(piece.shape[0], live_doc.shape[0], live_doc.shape[1])
    sims = jnp.where(live_doc[None], sims, -1e30)
    return jnp.max(sims, axis=2)


def on_device(
    tokens,
    attend_weight,
    output_weight,
    attend_gain,
    up_weight,
    down_weight,
    mlp_gain,
    embed_weight,
    query_length,
    documents,
    document_length,
    candidates,
):
    rows = tokens.shape[0]
    requests = query_length.shape[0]
    held_docs = documents.shape[0]
    packed = jnp.dot(tokens, attend_weight, preferred_element_type=jnp.float32).astype(jnp.bfloat16)
    packed = packed.reshape(requests, SEQ, 3, HEADS, HD)
    live_slot = jnp.arange(SEQ)[None, :] < query_length[:, None]
    logits = jnp.einsum(
        "rqhd,rkhd->rhqk", packed[:, :, 0], packed[:, :, 1], preferred_element_type=jnp.float32
    ) * HD ** (-0.5)
    logits = jnp.where(live_slot[:, None, None, :], logits, -1e30)
    highest = jnp.max(logits, axis=-1, keepdims=True)
    weights = jnp.exp(logits - highest)
    probs = (weights / jnp.sum(weights, axis=-1, keepdims=True)).astype(jnp.bfloat16)
    context = jnp.einsum(
        "rhqk,rkhd->rqhd", probs, packed[:, :, 2], preferred_element_type=jnp.float32
    )
    context = context.astype(jnp.bfloat16).reshape(rows, D)
    attended = jnp.dot(context, output_weight, preferred_element_type=jnp.float32)
    normed = norm_rows(tokens.astype(jnp.float32) + attended, attend_gain).astype(jnp.bfloat16)
    hidden = jax.nn.gelu(
        jnp.dot(
            normed,
            lax.all_gather(up_weight, "mlp", axis=1, tiled=True),
            preferred_element_type=jnp.float32,
        ),
        approximate=False,
    ).astype(jnp.bfloat16)
    reduced = lax.dot_general(
        hidden,
        lax.all_gather(down_weight, "mlp", axis=1, tiled=True),
        (((1,), (1,)), ((), ())),
        preferred_element_type=jnp.float32,
    )
    layer_out = norm_rows(normed.astype(jnp.float32) + reduced, mlp_gain).astype(jnp.bfloat16)
    projected = jnp.dot(layer_out, embed_weight, preferred_element_type=jnp.float32)
    unit = projected * lax.rsqrt(jnp.sum(projected * projected, axis=-1, keepdims=True) + 1e-06)
    embedded = jnp.where(live_slot.reshape(rows, 1), unit, 0.0).astype(jnp.bfloat16)
    shard_rows = documents.shape[1]
    positions = lax.axis_index("mlp") * shard_rows + jnp.arange(shard_rows)
    live_doc = positions[None, :] < document_length[:, None]
    flat_docs = documents.reshape(held_docs * shard_rows, P_SIZE)
    partial_best = best_match(
        lax.all_gather(embedded, ("req", "mlp"), axis=0, tiled=True), flat_docs, live_doc
    )
    best = lax.pmax(partial_best.astype(jnp.bfloat16), "mlp").astype(partial_best.dtype)
    totals = jnp.sum(best.reshape(best.shape[0] // SEQ, SEQ, held_docs), axis=1)
    swapped = lax.all_to_all(totals, "req", split_axis=0, concat_axis=1, tiled=True)
    swapped = lax.dynamic_slice_in_dim(swapped, lax.axis_index("mlp") * requests, requests, 0)
    all_docs = swapped.shape[1]
    matches = candidates[:, :, None] == jnp.arange(all_docs, dtype=jnp.int32)[None, None, :]
    scores = jnp.sum(jnp.where(matches, swapped[:, None, :], 0.0), axis=2)
    return (embedded, scores)


def solution(mesh):
    return jax.shard_map(
        on_device,
        mesh=mesh,
        in_specs=(
            P(("req", "mlp"), None),
            P(),
            P(),
            P(),
            P(None, "mlp"),
            P(None, "mlp"),
            P(),
            P(),
            P(("req", "mlp")),
            P("req", "mlp", None),
            P("req"),
            P(("req", "mlp"), None),
        ),
        out_specs=(P(("req", "mlp"), None), P(("req", "mlp"), None)),
        check_vma=False,
    )
```

profile of v0, /device:TPU:0, one launch (start us, length us, event | category | flops | bytes accessed | tf_op | source)
XLA Modules:
  0.0 354.3 jit_solution(13701282405548366960)
XLA Ops:
  7.2 0.0 copy-start
  7.2 0.0 all-gather.4.cloned.1.call-start
  7.2 0.7 all-gather.4.cloned.1.call-update
  7.9 0.0 all-gather.6.cloned.1.call-start
  8.0 0.7 all-gather.6.cloned.1.call-update
  8.7 0.0 all-gather.8.cloned.1.call-start
  8.7 8.2 %convolution_convert_fusion = bf16[512,3072]{1,0:T(8,128)(2,1)} fusion(bf16[512,1024]{1,0:T(8,128)(2,1)} %param.12, bf16[1024,3072]{1,0:T(8,128)(2,1)} %param.13), kind=kOutput, calls=%fused_computation.23 | convolution fusion | flops 3222798336 | bytes 10485760 | tf_op jit(solution)/shard_map/dot_general | solution.py:46
  17.0 8.8 %reshape.125 = bf16[4,128,3,16,64]{4,3,2,1,0:T(8,128)(2,1)} reshape(bf16[512,3072]{1,0:T(8,128)(2,1)} %convolution_convert_fusion) | data formatting | bytes 6291456 | tf_op jit(solution)/shard_map/reshape | solution.py:47
  25.7 0.0 copy-start.12
  25.7 6.1 %fusion.70 = (bf16[4,128,1,16,64]{4,3,2,1,0:T(8,128)(2,1)}, bf16[4,128,1,16,64]{4,3,2,1,0:T(8,128)(2,1)}, bf16[4,128,1,16,64]{4,3,2,1,0:T(8,128)(2,1)}) fusion(bf16[4,128,3,16,64]{4,3,2,1,0:T(8,128)(2,1)} %reshape.125), kind=kLoop, calls=%fused_computation.100 | loop fusion | bytes 6291456 | tf_op jit(solution)/shard_map/slice | solution.py:57
  31.8 2.8 copy.70
  34.7 3.5 %copy.71 = bf16[4,128,1,16,64]{1,4,3,0,2:T(8,128)(2,1)} copy(bf16[4,128,1,16,64]{4,3,2,1,0:T(8,128)(2,1)} %get-tuple-element.14) | data formatting | bytes 2097152
  38.2 3.7 %copy.69 = bf16[4,128,1,16,64]{1,4,3,0,2:T(8,128)(2,1)} copy(bf16[4,128,1,16,64]{4,3,2,1,0:T(8,128)(2,1)} %get-tuple-element.12) | data formatting | bytes 2097152
  41.9 0.0 copy-done.12
  41.9 0.1 fusion.68
  42.0 2.1 fusion.29
  44.1 1.7 fusion.71
  45.7 0.0 copy-done.4
  45.8 0.0 copy-start.5
  45.8 0.7 fusion.25
  46.5 0.0 copy-start.11
  46.5 0.9 copy.56
  47.4 0.0 copy-done
  47.4 0.0 copy-done.5
  47.4 1.4 fusion.72
  48.8 1.3 copy-done.2
  50.2 0.3 multiply_reduce_fusion.1
  50.5 0.0 copy-start.6
  50.5 0.0 copy-start.7
  50.5 0.0 copy-start.9
  50.5 0.0 copy-start.10
  50.6 11.3 %all-gather.4.cloned.1.call-done = bf16[1024,4096]{1,0:T(8,128)(2,1)} async-done(((bf16[1024,512]{1,0:T(8,128)(2,1)}), bf16[1024,4096]{1,0:T(8,128)(2,1)}) %all-gather.4.cloned.1.call-update) | async-done | bytes 8388624 | tf_op jit(solution)/shard_map/all_gather | solution.py:65
  61.9 51.6 %all-gather.6.cloned.1.call-done = bf16[1024,4096]{1,0:T(8,128)(2,1)} async-done(((bf16[1024,512]{1,0:T(8,128)(2,1)}), bf16[1024,4096]{1,0:T(8,128)(2,1)}) %all-gather.6.cloned.1.call-update) | async-done | bytes 8388624 | tf_op jit(solution)/shard_map/all_gather | solution.py:72
  113.5 0.0 copy-done.11
  113.5 32.1 %fusion.73 = (f32[512]{0:T(512)S(1)}, f32[512,1024]{1,0:T(8,128)S(1)}) fusion(bf16[1024,4096]{1,0:T(8,128)(2,1)} %all-gather.6.cloned.1.call-done, f32[1024]{0:T(1024)S(1)} %copy-done.11, f32[512]{0:T(512)S(1)} %add_rsqrt_fusion.2, f32[512,1024]{1,0:T(8,128)} %copy-done.2, f32[512]{0:T(512)S(1)} %broadcast_multiply_fusion.1, ...), kind=kOutput, calls=%fused_computation.103 | convolution fusion | flops 8732016640 | bytes 20981760 | tf_op jit(solution)/shard_map/dot_general | solution.py:70
  145.7 0.3 multiply_reduce_fusion
  146.0 0.0 copy-done.6
  146.0 0.0 copy-done.7
  146.0 0.7 multiply_reduce_fusion.2
  146.7 0.7 select_convert_fusion
  147.4 0.0 all-gather.8.cloned.1.call-update
  147.4 0.0 all-reduce.2.cloned.1.call-start
  147.5 0.0 copy-done.9
  147.5 0.1 broadcast_compare_fusion
  147.6 91.0 %all-gather.8.cloned.1.call-done = bf16[65536,128]{0,1:T(8,128)(2,1)} async-done(((bf16[512,128]{0,1:T(8,128)(2,1)}), bf16[65536,128]{0,1:T(8,128)(2,1)}) %all-gather.8.cloned.1.call-update) | async-done | bytes 16777232 | tf_op jit(solution)/shard_map/all_gather | solution.py:85
  238.6 0.0 copy-done.10
  238.6 27.4 %fusion.2 = bf16[65536,8]{0,1:T(8,128)(2,1)} fusion(bf16[8,32,128]{2,1,0:T(8,128)(2,1)S(1)} %copy-done.10, bf16[65536,128]{0,1:T(8,128)(2,1)} %all-gather.8.cloned.1.call-done, pred[8,32]{1,0:T(8,128)(4,1)S(1)} %broadcast_compare_fusion), kind=kOutput, calls=%fused_computation.4 | convolution fusion | flops 4327997440 | bytes 17891584 | tf_op jit(solution)/shard_map/dot_general | solution.py:21
  266.0 0.0 all-reduce.2.cloned.1.call-update
  266.0 62.4 %all-reduce.2.cloned.1.call-done = bf16[512,128,8]{1,2,0:T(8,128)(2,1)} async-done(((bf16[512,128,8]{1,2,0:T(8,128)(2,1)}), bf16[512,128,8]{1,2,0:T(8,128)(2,1)}) %all-reduce.2.cloned.1.call-update) | async-done | bytes 1048592 | tf_op jit(solution)/shard_map/pmax | solution.py:87
  328.4 1.8 convert_reduce_fusion
  330.2 0.1 copy.59
  330.3 0.7 reshape.127
  331.1 6.9 %all-to-all-start = ((f32[16,1,256]{2,1,0:T(1,128)}), f32[16,1,256]{2,1,0:T(1,128)S(1)}, u32[]{:S(2)}, u32[]{:S(2)}) async-start(f32[16,1,256]{2,1,0:T(1,128)} %reshape.127), calls=%async_computation | async-start | bytes 32768 | tf_op jit(solution)/shard_map/all_to_all | solution.py:89
  338.0 0.0 copy-done.3
  338.0 0.8 copy.61
  338.8 6.8 %all-to-all-done = f32[16,1,256]{2,1,0:T(1,128)S(1)} async-done(((f32[16,1,256]{2,1,0:T(1,128)}), f32[16,1,256]{2,1,0:T(1,128)S(1)}, u32[]{:S(2)}, u32[]{:S(2)}) %all-to-all-start) | async-done | bytes 16416 | tf_op jit(solution)/shard_map/all_to_all | solution.py:89
  345.6 0.5 broadcast.105
  346.1 0.7 reduce
  346.8 0.1 reshape.128
  346.9 0.1 constant_dynamic-slice_fusion
  347.0 0.1 copy.60
  347.0 0.0 copy-done.8
  347.0 0.8 select_reduce_fusion
  347.8 0.0 copy-done.1
  (12 shorter events, 0.0 us)
Async XLA Ops:
  7.2 40.2 %copy-start = (bf16[1024,1024]{1,0:T(8,128)(2,1)S(1)}, bf16[1024,1024]{1,0:T(8,128)(2,1)}, u32[]{:S(2)}) copy-start(bf16[1024,1024]{1,0:T(8,128)(2,1)} %param.14) | copy-start | bytes 6291460
  7.2 54.7 %all-gather.4.cloned.1.call-start = ((), (), s32[]{:S(2)}) async-start(), calls=%async_computation.1 | async-start | bytes 9437184 | tf_op jit(solution)/shard_map/all_gather | solution.py:65
  7.9 105.6 %all-gather.6.cloned.1.call-start = ((), (), s32[]{:S(2)}) async-start(), calls=%async_computation.2 | async-start | bytes 9437184 | tf_op jit(solution)/shard_map/all_gather | solution.py:72
  8.7 229.9 %all-gather.8.cloned.1.call-start = ((), (), s32[]{:S(2)}) async-start(), calls=%async_computation.3 | async-start | bytes 16908288 | tf_op jit(solution)/shard_map/all_gather | solution.py:85
  25.7 16.2 %copy-start.12 = (s32[4]{0:T(128)S(1)}, s32[4]{0:T(128)}, u32[]{:S(2)}) copy-start(s32[4]{0:T(128)} %param.20) | copy-start | bytes 52
  41.9 3.9 %copy-start.4 = (bf16[4,128,1,16,64]{1,4,3,0,2:T(8,128)(2,1)S(1)}, bf16[4,128,1,16,64]{1,4,3,0,2:T(8,128)(2,1)}, u32[]{:S(2)}) copy-start(bf16[4,128,1,16,64]{1,4,3,0,2:T(8,128)(2,1)} %copy.69) | copy-start | bytes 3145732
  45.8 1.7 copy-start.5
  46.5 67.0 %copy-start.11 = (f32[1024]{0:T(1024)S(1)}, f32[1024]{0:T(1024)}, u32[]{:S(2)}) copy-start(f32[1024]{0:T(1024)} %param.15) | copy-start | bytes 12292
  48.8 1.4 copy-start.2
  50.5 95.5 %copy-start.6 = (bf16[1024,128]{1,0:T(8,128)(2,1)S(1)}, bf16[1024,128]{1,0:T(8,128)(2,1)}, u32[]{:S(2)}) copy-start(bf16[1024,128]{1,0:T(8,128)(2,1)} %param.19) | copy-start | bytes 786436
  50.5 95.5 %copy-start.7 = (f32[1024]{0:T(1024)S(1)}, f32[1024]{0:T(1024)}, u32[]{:S(2)}) copy-start(f32[1024]{0:T(1024)} %param.18) | copy-start | bytes 12292
  50.5 97.0 %copy-start.9 = (s32[8]{0:T(128)S(1)}, s32[8]{0:T(128)}, u32[]{:S(2)}) copy-start(s32[8]{0:T(128)} %param.22) | copy-start | bytes 100
  50.5 188.0 %copy-start.10 = (bf16[8,32,128]{2,1,0:T(8,128)(2,1)S(1)}, bf16[8,32,128]{2,1,0:T(8,128)(2,1)}, u32[]{:S(2)}) copy-start(bf16[8,32,128]{2,1,0:T(8,128)(2,1)} %param.21) | copy-start | bytes 196612
  147.4 180.9 %all-reduce.2.cloned.1.call-start = ((), (), s32[]{:S(2)}) async-start(), calls=%async_computation.4 | async-start | bytes 2097152 | tf_op jit(solution)/shard_map/pmax | solution.py:87
  147.6 190.4 %copy-start.3 = (bf16[512,128]{0,1:T(8,128)(2,1)S(1)}, bf16[512,128]{0,1:T(8,128)(2,1)}, u32[]{:S(2)}) copy-start(bf16[512,128]{0,1:T(8,128)(2,1)} %select_convert_fusion) | copy-start | bytes 393220
  147.6 199.5 %copy-start.8 = (s32[4,8]{1,0:T(4,128)S(1)}, s32[4,8]{1,0:T(4,128)}, u32[]{:S(2)}) copy-start(s32[4,8]{1,0:T(4,128)} %param.23) | copy-start | bytes 388
  238.6 109.2 %copy-start.1 = (bf16[1024,1024]{1,0:T(8,128)(2,1)S(1)}, bf16[1024,1024]{1,0:T(8,128)(2,1)}, u32[]{:S(2)}) copy-start(bf16[1024,1024]{1,0:T(8,128)(2,1)} %param.14) | copy-start | bytes 6291460
  331.1 14.5 %all-to-all-start = ((f32[16,1,256]{2,1,0:T(1,128)}), f32[16,1,256]{2,1,0:T(1,128)S(1)}, u32[]{:S(2)}, u32[]{:S(2)}) async-start(f32[16,1,256]{2,1,0:T(1,128)} %reshape.127), calls=%async_computation | async-start | bytes 32768 | tf_op jit(solution)/shard_map/all_to_all | solution.py:89
Sparse Core Ops, SparseCore 0:
  9.7 52.1 all-gather.3
  63.6 49.8 all-gather.5
  147.5 90.9 all-gather.7
  266.1 62.1 all-reduce.1
where the time goes:
time: 355 us; the launch traced here: 354 us
  waiting for transfers between devices  225 us (63%)
  matrix products  72.6 us (20%)
  local copies, waits for them, and re-layouts  29.5 us (8%)
  between operations  14 us (4%)
  starting transfers between devices  7.1 us (2%)
  other arithmetic  6.53 us (2%)
    all_gather x1, waiting for transfers between devices, on_device(): lax.all_gather(embedded, ('req', 'mlp'), axis=0, tiled=True)  91 us
    pmax x1, waiting for transfers between devices, on_device(): lax.pmax(partial_best.astype(jnp.bfloat16), 'mlp')  62.4 us
    all_gather x1, waiting for transfers between devices, on_device(): lax.all_gather(down_weight, 'mlp', axis=1, tiled=True)  51.6 us
    dot_general x1, matrix products, on_device(): lax.dot_general(hidden, lax.all_gather(down_weight, 'mlp', axis=1, tiled=...  32.1 us
    dot_general x1, matrix products, best_match(): lax.dot_general(piece, flat_docs, (((1,), (1,)), ((), ())), preferred_ele...  27.4 us
    unnamed x32, local copies, waits for them, and re-layouts  13 us
    all_gather x1, waiting for transfers between devices, on_device(): lax.all_gather(up_weight, 'mlp', axis=1, tiled=True)  11.3 us
    reshape x1, local copies, waits for them, and re-layouts, on_device(): packed = packed.reshape(requests, SEQ, 3, HEADS, HD)  8.77 us
  transfers between devices with their start and end apart: 5, of which 5 were waited for; matrix products, arithmetic and copies ran while one was open for 12% of the time, Pallas kernels for 0%

commit v1 on v0

--- a/solution.py
+++ b/solution.py
@@ -69,7 +69,9 @@
     ).astype(jnp.bfloat16)
     reduced = lax.dot_general(
         hidden,
-        lax.all_gather(down_weight, "mlp", axis=1, tiled=True),
+        jnp.concatenate(
+            lax.all_to_all(jnp.stack([down_weight] * lax.axis_size("mlp")), "mlp", 0, 0), axis=1
+        ),
         (((1,), (1,)), ((), ())),
         preferred_element_type=jnp.float32,
     )

time: 355 us -> 389 us (1.096)
  waiting for transfers between devices: 225 us -> 248 us
  local copies, waits for them, and re-layouts: 29.5 us -> 35.1 us
  starting transfers between devices: 7.1 us -> 12.2 us
    all_to_all x0 -> x1, waiting for transfers between devices: none -> 87.1 us  [on_device(): lax.all_to_all(jnp.stack([down_weight] * lax.axis_size('mlp')), 'mlp', 0, 0)]
    all_gather x1 -> x0, waiting for transfers between devices: 51.6 us -> none  [on_device(): lax.all_gather(down_weight, 'mlp', axis=1, tiled=True)]
    all_gather x1, waiting for transfers between devices: 11.3 us -> 0.01 us  [on_device(): lax.all_gather(up_weight, 'mlp', axis=1, tiled=True)]
    all_to_all x0 -> x1, starting transfers between devices: none -> 5.17 us  [on_device(): lax.all_to_all(jnp.stack([down_weight] * lax.axis_size('mlp')), 'mlp', 0, 0)]
    another operation x0 -> x1, local copies, waits for them, and re-layouts: none -> 4.31 us  [on_device(): jnp.stack([down_weight] * lax.axis_size('mlp'))]
    unnamed x32 -> x35, local copies, waits for them, and re-layouts: 13 us -> 14.4 us
  transfers between devices with their start and end apart: 5 -> 5, of which waited for: 5 -> 4; matrix products, arithmetic and copies ran while one was open for 12% -> 12% of each run, Pallas kernels for 0% -> 0%
where the time goes in v1:
time: 389 us
  waiting for transfers between devices  248 us (64%)
  matrix products  72.5 us (19%)
  local copies, waits for them, and re-layouts  35.1 us (9%)
  between operations  14 us (4%)
  starting transfers between devices  12.2 us (3%)
  other arithmetic  6.53 us (2%)
    all_gather x1, waiting for transfers between devices, on_device(): lax.all_gather(embedded, ('req', 'mlp'), axis=0, tiled=True)  91.3 us
    all_to_all x1, waiting for transfers between devices, on_device(): lax.all_to_all(jnp.stack([down_weight] * lax.axis_size('mlp')), 'mlp', 0, 0)  87.1 us
    pmax x1, waiting for transfers between devices, on_device(): lax.pmax(partial_best.astype(jnp.bfloat16), 'mlp')  62.4 us
    dot_general x1, matrix products, on_device(): lax.dot_general(hidden, jnp.concatenate(lax.all_to_all(jnp.stack([down_we...  32.4 us
    dot_general x1, matrix products, best_match(): lax.dot_general(piece, flat_docs, (((1,), (1,)), ((), ())), preferred_ele...  27.4 us
    unnamed x35, local copies, waits for them, and re-layouts  14.4 us
    reshape x1, local copies, waits for them, and re-layouts, on_device(): packed = packed.reshape(requests, SEQ, 3, HEADS, HD)  8.61 us
    dot_general x1, matrix products, on_device(): jnp.dot(tokens, attend_weight, preferred_element_type=jnp.float32)  7.86 us
  transfers between devices with their start and end apart: 5, of which 4 were waited for; matrix products, arithmetic and copies ran while one was open for 12% of the time, Pallas kernels for 0%

profile of v1, /device:TPU:0, one launch (start us, length us, event | category | flops | bytes accessed | tf_op | source)
XLA Modules:
  0.0 388.6 jit_solution(17180622559967837678)
XLA Ops:
  7.2 0.0 copy-start
  7.2 0.0 all-gather.3.cloned.1.call-start
  7.2 0.7 all-gather.3.cloned.1.call-update
  7.9 1.5 copy.60
  9.4 4.3 %stack.2 = bf16[8,1024,512]{1,2,0:T(8,128)(2,1)} broadcast(bf16[1024,512]{0,1:T(8,128)(2,1)S(1)} %copy.60), dimensions={1,2} | broadcast | bytes 9437184 | tf_op jit(solution)/shard_map/stack | solution.py:73
  13.7 0.0 copy-start.5
  13.7 5.2 %all-to-all-start = ((bf16[8,1024,512]{1,2,0:T(8,128)(2,1)}), bf16[8,1024,512]{1,2,0:T(8,128)(2,1)}, u32[]{:S(2)}, u32[]{:S(2)}) async-start(bf16[8,1024,512]{1,2,0:T(8,128)(2,1)} %stack.2), calls=%async_computation | async-start | bytes 16777216 | tf_op jit(solution)/shard_map/all_to_all | solution.py:73
  18.9 0.0 all-gather.5.cloned.1.call-start
  18.9 0.0 copy-done.5
  19.0 7.9 %convolution_convert_fusion = bf16[512,3072]{1,0:T(8,128)(2,1)} fusion(bf16[512,1024]{1,0:T(8,128)(2,1)S(1)} %copy-done.5, bf16[1024,3072]{1,0:T(8,128)(2,1)} %param.13), kind=kOutput, calls=%fused_computation.23 | convolution fusion | flops 3222798336 | bytes 10485760 | tf_op jit(solution)/shard_map/dot_general | solution.py:46
  26.8 8.6 %reshape.135 = bf16[4,128,3,16,64]{4,3,2,1,0:T(8,128)(2,1)} reshape(bf16[512,3072]{1,0:T(8,128)(2,1)} %convolution_convert_fusion) | data formatting | bytes 6291456 | tf_op jit(solution)/shard_map/reshape | solution.py:47
  35.4 0.0 copy-start.13
  35.4 6.0 %fusion.70 = (bf16[4,128,1,16,64]{4,3,2,1,0:T(8,128)(2,1)}, bf16[4,128,1,16,64]{4,3,2,1,0:T(8,128)(2,1)}, bf16[4,128,1,16,64]{4,3,2,1,0:T(8,128)(2,1)}) fusion(bf16[4,128,3,16,64]{4,3,2,1,0:T(8,128)(2,1)} %reshape.135), kind=kLoop, calls=%fused_computation.100 | loop fusion | bytes 6291456 | tf_op jit(solution)/shard_map/slice | solution.py:57
  41.5 2.8 copy.74
  44.3 3.6 copy.75
  47.9 3.5 copy.73
  51.4 0.0 copy-done.13
  51.4 0.1 fusion.68
  51.5 2.1 fusion.29
  53.6 1.7 fusion.71
  55.3 0.0 copy-done.4
  55.3 0.0 copy-start.6
  55.3 0.7 fusion.25
  56.0 0.0 copy-start.12
  56.0 0.9 copy.59
  56.9 0.0 copy-done
  56.9 0.0 copy-done.6
  57.0 1.4 fusion.72
  58.4 1.4 copy-done.2
  59.7 0.3 multiply_reduce_fusion.1
  60.1 87.1 %all-to-all-done = bf16[8,1024,512]{1,2,0:T(8,128)(2,1)} async-done(((bf16[8,1024,512]{1,2,0:T(8,128)(2,1)}), bf16[8,1024,512]{1,2,0:T(8,128)(2,1)}, u32[]{:S(2)}, u32[]{:S(2)}) %all-to-all-start) | async-done | bytes 8388640 | tf_op jit(solution)/shard_map/all_to_all | solution.py:73
  147.2 0.0 copy-done.12
  147.2 0.0 copy-start.10
  147.2 0.0 copy-start.11
  147.3 32.4 %fusion.73 = (f32[512]{0:T(512)S(1)}, f32[512,1024]{1,0:T(8,128)S(1)}) fusion(bf16[1024,4096]{0,1:T(8,128)(2,1)} %bitcast.6, f32[1024]{0:T(1024)S(1)} %copy-done.12, f32[512]{0:T(512)S(1)} %add_rsqrt_fusion.2, f32[512,1024]{1,0:T(8,128)} %copy-done.2, f32[512]{0:T(512)S(1)} %broadcast_multiply_fusion.1, bf16[1024,4096]{1,0:T(8,128)(2,1)} %all-gather.3.cloned.1.call-done), kind=kOutput, calls=%fused_computation.103 | convolution fusion | flops 8732016640 | bytes 20981760 | tf_op jit(solution)/shard_map/dot_general | solution.py:70
  179.7 0.3 multiply_reduce_fusion
  180.0 0.0 copy-done.7
  180.0 0.0 copy-done.8
  180.0 0.7 multiply_reduce_fusion.2
  180.7 0.7 select_convert_fusion
  181.4 0.0 all-gather.5.cloned.1.call-update
  181.4 0.0 all-reduce.2.cloned.1.call-start
  181.5 0.0 copy-done.10
  181.5 0.1 broadcast_compare_fusion
  181.6 91.3 %all-gather.5.cloned.1.call-done = bf16[65536,128]{0,1:T(8,128)(2,1)} async-done(((bf16[512,128]{0,1:T(8,128)(2,1)}), bf16[65536,128]{0,1:T(8,128)(2,1)}) %all-gather.5.cloned.1.call-update) | async-done | bytes 16777232 | tf_op jit(solution)/shard_map/all_gather | solution.py:87
  272.8 0.0 copy-done.11
  272.8 27.4 %fusion.2 = bf16[65536,8]{0,1:T(8,128)(2,1)} fusion(bf16[8,32,128]{2,1,0:T(8,128)(2,1)S(1)} %copy-done.11, bf16[65536,128]{0,1:T(8,128)(2,1)} %all-gather.5.cloned.1.call-done, pred[8,32]{1,0:T(8,128)(4,1)S(1)} %broadcast_compare_fusion), kind=kOutput, calls=%fused_computation.4 | convolution fusion | flops 4327997440 | bytes 17891584 | tf_op jit(solution)/shard_map/dot_general | solution.py:21
  300.3 0.0 all-reduce.2.cloned.1.call-update
  300.3 62.4 %all-reduce.2.cloned.1.call-done = bf16[512,128,8]{1,2,0:T(8,128)(2,1)} async-done(((bf16[512,128,8]{1,2,0:T(8,128)(2,1)}), bf16[512,128,8]{1,2,0:T(8,128)(2,1)}) %all-reduce.2.cloned.1.call-update) | async-done | bytes 1048592 | tf_op jit(solution)/shard_map/pmax | solution.py:89
  362.6 1.8 convert_reduce_fusion
  364.5 0.1 copy.63
  364.6 0.7 reshape.137
  365.3 6.9 %all-to-all-start.1 = ((f32[16,1,256]{2,1,0:T(1,128)}), f32[16,1,256]{2,1,0:T(1,128)S(1)}, u32[]{:S(2)}, u32[]{:S(2)}) async-start(f32[16,1,256]{2,1,0:T(1,128)} %reshape.137), calls=%async_computation.1 | async-start | bytes 32768 | tf_op jit(solution)/shard_map/all_to_all | solution.py:91
  372.3 0.0 copy-done.3
  372.3 0.8 copy.65
  373.0 6.8 %all-to-all-done.1 = f32[16,1,256]{2,1,0:T(1,128)S(1)} async-done(((f32[16,1,256]{2,1,0:T(1,128)}), f32[16,1,256]{2,1,0:T(1,128)S(1)}, u32[]{:S(2)}, u32[]{:S(2)}) %all-to-all-start.1) | async-done | bytes 16416 | tf_op jit(solution)/shard_map/all_to_all | solution.py:91
  379.9 0.5 broadcast.107
  380.4 0.7 reduce
  381.1 0.1 reshape.138
  381.1 0.1 constant_dynamic-slice_fusion
  381.2 0.1 copy.64
  381.3 0.0 copy-done.9
  381.3 0.8 select_reduce_fusion
  382.1 0.0 copy-done.1
  (15 shorter events, 0.1 us)
Async XLA Ops:
  7.2 49.8 %copy-start = (bf16[1024,1024]{1,0:T(8,128)(2,1)S(1)}, bf16[1024,1024]{1,0:T(8,128)(2,1)}, u32[]{:S(2)}) copy-start(bf16[1024,1024]{1,0:T(8,128)(2,1)} %param.14) | copy-start | bytes 6291460
  7.2 140.0 %all-gather.3.cloned.1.call-start = ((), (), s32[]{:S(2)}) async-start(), calls=%async_computation.2 | async-start | bytes 9437184 | tf_op jit(solution)/shard_map/all_gather | solution.py:65
  13.7 5.2 %copy-start.5 = (bf16[512,1024]{1,0:T(8,128)(2,1)S(1)}, bf16[512,1024]{1,0:T(8,128)(2,1)}, u32[]{:S(2)}) copy-start(bf16[512,1024]{1,0:T(8,128)(2,1)} %param.12) | copy-start | bytes 3145732
  13.7 133.5 %all-to-all-start = ((bf16[8,1024,512]{1,2,0:T(8,128)(2,1)}), bf16[8,1024,512]{1,2,0:T(8,128)(2,1)}, u32[]{:S(2)}, u32[]{:S(2)}) async-start(bf16[8,1024,512]{1,2,0:T(8,128)(2,1)} %stack.2), calls=%async_computation | async-start | bytes 16777216 | tf_op jit(solution)/shard_map/all_to_all | solution.py:73
  18.9 253.9 %all-gather.5.cloned.1.call-start = ((), (), s32[]{:S(2)}) async-start(), calls=%async_computation.3 | async-start | bytes 16908288 | tf_op jit(solution)/shard_map/all_gather | solution.py:87
  35.4 16.0 %copy-start.13 = (s32[4]{0:T(128)S(1)}, s32[4]{0:T(128)}, u32[]{:S(2)}) copy-start(s32[4]{0:T(128)} %param.20) | copy-start | bytes 52
  51.4 3.8 copy-start.4
  55.3 1.7 copy-start.6
  56.0 91.2 %copy-start.12 = (f32[1024]{0:T(1024)S(1)}, f32[1024]{0:T(1024)}, u32[]{:S(2)}) copy-start(f32[1024]{0:T(1024)} %param.15) | copy-start | bytes 12292
  58.3 1.4 copy-start.2
  147.2 32.8 %copy-start.7 = (bf16[1024,128]{1,0:T(8,128)(2,1)S(1)}, bf16[1024,128]{1,0:T(8,128)(2,1)}, u32[]{:S(2)}) copy-start(bf16[1024,128]{1,0:T(8,128)(2,1)} %param.19) | copy-start | bytes 786436
  147.2 32.8 %copy-start.8 = (f32[1024]{0:T(1024)S(1)}, f32[1024]{0:T(1024)}, u32[]{:S(2)}) copy-start(f32[1024]{0:T(1024)} %param.18) | copy-start | bytes 12292
  147.2 34.3 %copy-start.10 = (s32[8]{0:T(128)S(1)}, s32[8]{0:T(128)}, u32[]{:S(2)}) copy-start(s32[8]{0:T(128)} %param.22) | copy-start | bytes 100
  147.2 125.6 %copy-start.11 = (bf16[8,32,128]{2,1,0:T(8,128)(2,1)S(1)}, bf16[8,32,128]{2,1,0:T(8,128)(2,1)}, u32[]{:S(2)}) copy-start(bf16[8,32,128]{2,1,0:T(8,128)(2,1)} %param.21) | copy-start | bytes 196612
  181.4 181.2 %all-reduce.2.cloned.1.call-start = ((), (), s32[]{:S(2)}) async-start(), calls=%async_computation.4 | async-start | bytes 2097152 | tf_op jit(solution)/shard_map/pmax | solution.py:89
  181.6 190.7 %copy-start.3 = (bf16[512,128]{0,1:T(8,128)(2,1)S(1)}, bf16[512,128]{0,1:T(8,128)(2,1)}, u32[]{:S(2)}) copy-start(bf16[512,128]{0,1:T(8,128)(2,1)} %select_convert_fusion) | copy-start | bytes 393220
  181.6 199.7 %copy-start.9 = (s32[4,8]{1,0:T(4,128)S(1)}, s32[4,8]{1,0:T(4,128)}, u32[]{:S(2)}) copy-start(s32[4,8]{1,0:T(4,128)} %param.23) | copy-start | bytes 388
  272.8 109.2 %copy-start.1 = (bf16[1024,1024]{1,0:T(8,128)(2,1)S(1)}, bf16[1024,1024]{1,0:T(8,128)(2,1)}, u32[]{:S(2)}) copy-start(bf16[1024,1024]{1,0:T(8,128)(2,1)} %param.14) | copy-start | bytes 6291460
  365.3 14.5 %all-to-all-start.1 = ((f32[16,1,256]{2,1,0:T(1,128)}), f32[16,1,256]{2,1,0:T(1,128)S(1)}, u32[]{:S(2)}, u32[]{:S(2)}) async-start(f32[16,1,256]{2,1,0:T(1,128)} %reshape.137), calls=%async_computation.1 | async-start | bytes 32768 | tf_op jit(solution)/shard_map/all_to_all | solution.py:91
Sparse Core Ops, SparseCore 0:
  9.7 96.4 all-gather.2
  181.5 91.2 all-gather.4
  300.4 62.1 all-reduce.1
